TPU v7x, 256 devices: a whole 4x4x8 slice. The times are simulated.
256 devices in a mesh: row: 16 (over z_hi, y, core), col: 16 (over z_lo, x).
Axes of the slice: x: 4, y: 4, z: 8 (z_hi: 2, z_lo: 4; z = z_hi * 4 + z_lo), core: 2. Of those that a mesh axis runs over, the one named last changes fastest.
Arguments:
- features: bfloat16 [65536, 128], P(('col', 'row')), may hold values from -6 to 6
- weight: bfloat16 [128, 128], replicated, may hold values from -0.5 to 0.5
- tiles: bfloat16 [16, 16, 352, 128, 128], P('row', 'col'), may hold values from -0.0546875 to 0.0546875
- tile_slots: int32 [16, 16, 352], P('row', 'col'), may hold values from 0 to 1023, as said below
- tile_counts: int32 [16, 16], P('row', 'col'), may hold values from 44 to 352, as said below
- cotangent: bfloat16 [65536, 128], P(('row', 'col')), may hold values from -6 to 6
Outputs:
- hidden: bfloat16 [65536, 128], P(('row', 'col'))
- feature_grad: bfloat16 [65536, 128], P(('col', 'row'))
- weight_grad: float32 [128, 128], replicated
Inputs may be any that keep to these rules, and one draw needn't show every extreme that they name: `tile_slots`: the slots of one block are distinct. `tile_counts`: some block has all 352 slots live.
All inputs are finite; a program needn't handle non-finite values.
Results may differ from a plain program's by a relative error of at most 0.006.
Values may be sent and summed in bfloat16 or wider, within the bound.
A program may use at most 128 MiB of HBM per device.

v0:
```python
import math
import jax
import jax.numpy as jnp
from jax import lax
from jax.sharding import PartitionSpec as P


def silu_grad(values):
    sig = jax.nn.sigmoid(values)
    return sig * (1.0 + values * (1.0 - sig))


def body(features, weight, tiles, tile_slots, tile_counts, cotangent):
    tile_vals = tiles[0, 0]
    slot_ids = tile_slots[0, 0]
    live_count = tile_counts[0, 0]
    tile_size = tile_vals.shape[-1]
    share_rows = features.shape[0]
    width = features.shape[1]
    slot_total = slot_ids.shape[0]
    row_count = lax.axis_size("row")
    col_count = lax.axis_size("col")
    tile_rows = share_rows * col_count // tile_size
    tile_cols = share_rows * row_count // tile_size
    col_index = lax.axis_index("col")
    projected = jnp.dot(features, weight, preferred_element_type=jnp.float32).astype(jnp.bfloat16)
    proj_block = lax.all_gather(projected, "row", axis=0, tiled=True)
    is_live = jnp.arange(slot_total, dtype=jnp.int32) < live_count
    gathered = proj_block.reshape(tile_cols, tile_size, width)[slot_ids % tile_cols]
    products = jnp.einsum("tij,tjf->tif", tile_vals, gathered, preferred_element_type=jnp.float32)
    fwd_targets = jnp.where(is_live, slot_ids // tile_cols, tile_rows)
    partial_value = jax.ops.segment_sum(products, fwd_targets, tile_rows + 1)[:tile_rows].reshape(
        tile_rows * tile_size, width
    )
    summed = lax.psum(partial_value, "col")
    own_rows = lax.dynamic_slice_in_dim(summed, col_index * share_rows, share_rows, 0)
    hidden = jax.nn.silu(own_rows).astype(jnp.bfloat16)
    cot_block = lax.all_gather(cotangent, "col", axis=0, tiled=True)
    grad_block = (cot_block.astype(jnp.float32) * silu_grad(summed)).astype(jnp.bfloat16)
    grad_tiles = grad_block.reshape(tile_rows, tile_size, width)[slot_ids // tile_cols]
    back_products = jnp.einsum(
        "tji,tjf->tif", tile_vals, grad_tiles, preferred_element_type=jnp.float32
    )
    back_targets = jnp.where(is_live, slot_ids % tile_cols, tile_cols)
    back_partial = jax.ops.segment_sum(back_products, back_targets, tile_cols + 1)[
        :tile_cols
    ].reshape(tile_cols * tile_size, width)
    grad_proj = lax.psum_scatter(back_partial, "row", scatter_dimension=0, tiled=True).astype(
        jnp.bfloat16
    )
    feature_grad = jnp.dot(grad_proj, weight.T, preferred_element_type=jnp.float32).astype(
        jnp.bfloat16
    )
    weight_term = jnp.dot(features.T, grad_proj, preferred_element_type=jnp.float32)
    node_total = share_rows * row_count * col_count
    weight_grad = lax.psum(weight_term, ("row", "col")) / math.sqrt(node_total)
    return (hidden, feature_grad, weight_grad)


def solution(mesh):
    placed = (
        P(("col", "row"), None),
        P(),
        P("row", "col", None, None, None),
        P("row", "col", None),
        P("row", "col"),
        P(("row", "col"), None),
    )
    return jax.shard_map(
        body,
        mesh=mesh,
        in_specs=placed,
        out_specs=(P(("row", "col"), None), P(("col", "row"), None), P()),
        check_vma=False,
    )
```

profile of v0, /device:TPU:1, one launch (start us, length us, event | category | flops | bytes accessed | tf_op | source)
XLA Modules:
  0.0 771.6 jit_solution(9133756063964806921)
XLA Ops:
  7.2 0.8 copy-done
  8.0 1.5 convolution_convert_fusion.1
  11.0 0.7 fusion.15
  11.7 0.7 fusion.13
  12.4 58.8 %all-gather.3.cloned.1.call-done = bf16[4096,128]{1,0:T(8,128)(2,1)} async-done(((bf16[256,128]{1,0:T(8,128)(2,1)}), bf16[4096,128]{1,0:T(8,128)(2,1)}) %all-gather.3.cloned.1.call-update) | async-done | bytes 1048592 | tf_op jit(solution)/shard_map/all_gather | solution.py:27
  71.3 12.2 %gather_fusion = bf16[352,128,128]{2,1,0:T(8,128)(2,1)} fusion(bf16[32,128,128]{2,1,0:T(8,128)(2,1)} %bitcast.41, s32[1024]{0:T(1024)S(1)} %pad_clamp_fusion.1), kind=kCustom, calls=%fused_computation | custom fusion | bytes 23070080 | tf_op jit(solution)/shard_map/gather | solution.py:29
  83.5 20.6 %fusion.4 = f32[352,128,128]{1,2,0:T(8,128)} fusion(bf16[352,128,128]{2,1,0:T(8,128)(2,1)} %gather_fusion, bf16[1,1,352,128,128]{4,3,2,1,0:T(8,128)(2,1)} %param.8), kind=kOutput, calls=%fused_computation.8 | convolution fusion | flops 1476395008 | bytes 46137344 | tf_op jit(solution)/shard_map/tij,tjf->tif/dot_general | solution.py:30
  104.1 23.5 %copy.13 = f32[352,128,128]{2,1,0:T(8,128)} copy(f32[352,128,128]{1,2,0:T(8,128)} %fusion.4) | data formatting | bytes 46137344 | tf_op jit(solution)/shard_map/tij,tjf->tif/dot_general | solution.py:30
  127.8 46.0 %scatter_fusion = f32[33,128,128]{2,1,0:T(8,128)S(1)} fusion(f32[33,128,128]{2,1,0:T(8,128)S(1)} %broadcast.191.clone, s32[352]{0:T(512)S(1)} %get-tuple-element.10, f32[352,128,128]{2,1,0:T(8,128)} %copy.13), kind=kCustom, calls=%fused_computation.2 | custom fusion | flops 5767168 | bytes 69207424 | tf_op jit(solution)/shard_map/scatter-add | solution.py:32
  173.9 1.5 slice.12
  175.7 153.0 %all-reduce.3.cloned.1.call-done = f32[4096,128]{1,0:T(8,128)} async-done(((f32[4096,128]{1,0:T(8,128)}), f32[4096,128]{1,0:T(8,128)}) %all-reduce.3.cloned.1.call-update) | async-done | bytes 2097168 | tf_op jit(solution)/shard_map/psum | solution.py:35
  328.6 2.6 multiply_convert_fusion
  331.3 11.0 %gather_fusion.1 = bf16[352,128,128]{2,1,0:T(8,128)(2,1)} fusion(bf16[32,128,128]{2,1,0:T(8,128)(2,1)S(1)} %bitcast.40, s32[1024]{0:T(1024)S(1)} %pad_clamp_fusion), kind=kCustom, calls=%fused_computation.1 | custom fusion | bytes 23070080 | tf_op jit(solution)/shard_map/gather | solution.py:40
  342.3 14.4 %fusion.7 = f32[352,128,128]{1,2,0:T(8,128)} fusion(bf16[352,128,128]{2,1,0:T(8,128)(2,1)} %gather_fusion.1, bf16[1,1,352,128,128]{4,3,2,1,0:T(8,128)(2,1)} %param.8), kind=kOutput, calls=%fused_computation.9 | convolution fusion | flops 1476395008 | bytes 46137344 | tf_op jit(solution)/shard_map/tji,tjf->tif/dot_general | solution.py:41
  356.7 23.5 %copy.15 = f32[352,128,128]{2,1,0:T(8,128)} copy(f32[352,128,128]{1,2,0:T(8,128)} %fusion.7) | data formatting | bytes 46137344 | tf_op jit(solution)/shard_map/tji,tjf->tif/dot_general | solution.py:41
  380.4 46.0 %scatter_fusion.1 = f32[33,128,128]{2,1,0:T(8,128)S(1)} fusion(f32[33,128,128]{2,1,0:T(8,128)S(1)} %broadcast.191, s32[352]{0:T(512)S(1)} %get-tuple-element.11, f32[352,128,128]{2,1,0:T(8,128)} %copy.15), kind=kCustom, calls=%fused_computation.3 | custom fusion | flops 5767168 | bytes 69207424 | tf_op jit(solution)/shard_map/scatter-add | solution.py:45
  426.4 1.5 slice.13
  428.0 1.6 multiply_convert_fusion.1
  429.6 92.6 %reduce-scatter.2.cloned.1.call-done = f32[256,128]{1,0:T(8,128)} async-done(((f32[4096,128]{1,0:T(8,128)}), f32[256,128]{1,0:T(8,128)}) %reduce-scatter.2.cloned.1.call-update) | async-done | bytes 131088 | tf_op jit(solution)/shard_map/reduce_scatter | solution.py:48
  522.2 1.7 convolution_bitcast_fusion
  524.0 1.7 convolution_convert_fusion
  525.7 237.9 %all-reduce.5.cloned.1.call-done = f32[128,128]{0,1:T(8,128)} async-done(((f32[128,128]{0,1:T(8,128)}), f32[128,128]{0,1:T(8,128)}) %all-reduce.5.cloned.1.call-update) | async-done | bytes 65552 | tf_op jit(solution)/shard_map/psum | solution.py:56
  763.5 0.8 broadcast_multiply_fusion
  764.4 0.7 copy.16
  (18 shorter events, 1.7 us)
Async XLA Ops:
  7.2 0.8 copy-start
  7.2 64.1 %all-gather.3.cloned.1.call-start = ((), (), s32[]{:S(2)}) async-start(), calls=%async_computation.1 | async-start | bytes 1114112 | tf_op jit(solution)/shard_map/all_gather | solution.py:27
  9.6 166.1 %all-gather.5.cloned.1.call-start = ((), (), s32[]{:S(2)}) async-start(), calls=%async_computation.3 | async-start | bytes 1114112 | tf_op jit(solution)/shard_map/all_gather | solution.py:38
  10.3 318.3 %all-reduce.3.cloned.1.call-start = ((), (), s32[]{:S(2)}) async-start(), calls=%async_computation.2 | async-start | bytes 4194304 | tf_op jit(solution)/shard_map/psum | solution.py:35
  175.4 346.8 %reduce-scatter.2.cloned.1.call-start = ((), (), s32[]{:S(2)}) async-start(), calls=%async_computation.4 | async-start | bytes 2228224 | tf_op jit(solution)/shard_map/reduce_scatter | solution.py:48
  380.4 143.5 %copy-start.1 = (bf16[128,128]{1,0:T(8,128)(2,1)S(1)}, bf16[128,128]{1,0:T(8,128)(2,1)}, u32[]{:S(2)}) copy-start(bf16[128,128]{1,0:T(8,128)(2,1)} %param.7) | copy-start | bytes 98308
  428.0 335.5 %all-reduce.5.cloned.1.call-start = ((), (), s32[]{:S(2)}) async-start(), calls=%async_computation.5 | async-start | bytes 131072 | tf_op jit(solution)/shard_map/psum | solution.py:56
Sparse Core Ops, SparseCore 0:
  11.3 59.9 all-gather.2
  73.1 65.9 all-gather.4
  175.5 153.0 all-reduce.2
  428.1 94.0 reduce-scatter.1
  528.1 235.3 all-reduce.4
where the time goes:
time: 774 us; the launch traced here: 772 us
  waiting for transfers between devices  543 us (70%)
  other arithmetic  98.5 us (13%)
  local copies, waits for them, and re-layouts  75.1 us (10%)
  matrix products  40 us (5%)
  between operations  14.5 us (2%)
    psum x1, waiting for transfers between devices, body(): weight_grad = lax.psum(weight_term, ('row', 'col')) / math.sqrt(node_total)  238 us
    psum x1, waiting for transfers between devices, body(): summed = lax.psum(partial_value, 'col')  153 us
    reduce_scatter x1, waiting for transfers between devices, body(): lax.psum_scatter(back_partial, 'row', scatter_dimension=0, tiled=True)  92.6 us
    all_gather x1, waiting for transfers between devices, body(): proj_block = lax.all_gather(projected, 'row', axis=0, tiled=True)  58.8 us
    scatter-add x1, other arithmetic, body(): jax.ops.segment_sum(products, fwd_targets, tile_rows + 1)[:tile_rows]  46 us
    scatter-add x1, other arithmetic, body(): jax.ops.segment_sum(back_products, back_targets, tile_cols + 1)[:tile_cols]  46 us
    dot_general x1, local copies, waits for them, and re-layouts, body(): jnp.einsum('tij,tjf->tif', tile_vals, gathered, preferred_element_type=jn...  23.5 us
    dot_general x1, local copies, waits for them, and re-layouts, body(): jnp.einsum('tji,tjf->tif', tile_vals, grad_tiles, preferred_element_type=...  23.5 us
  transfers between devices with their start and end apart: 5, of which 4 were waited for; matrix products, arithmetic and copies ran while one was open for 14% of the time, Pallas kernels for 0%

commit v1 on v0

--- a/solution.py
+++ b/solution.py
@@ -11,6 +11,10 @@
 
 
 def body(features, weight, tiles, tile_slots, tile_counts, cotangent):
+
+    def stacks_all_resolve(patch, dev_axis, ax_name):
+        return lax.psum(lax.psum(patch, axis_name=dev_axis), axis_name=ax_name)
+
     tile_vals = tiles[0, 0]
     slot_ids = tile_slots[0, 0]
     live_count = tile_counts[0, 0]
@@ -53,7 +57,7 @@
     )
     weight_term = jnp.dot(features.T, grad_proj, preferred_element_type=jnp.float32)
     node_total = share_rows * row_count * col_count
-    weight_grad = lax.psum(weight_term, ("row", "col")) / math.sqrt(node_total)
+    weight_grad = stacks_all_resolve(weight_term, "col", "row") / math.sqrt(node_total)
     return (hidden, feature_grad, weight_grad)
 
 

time: 774 us -> 847 us (1.094)
  waiting for transfers between devices: 543 us -> 614 us
    psum x1 -> x2, waiting for transfers between devices: 238 us -> 308 us  [stacks_all_resolve(): return lax.psum(lax.psum(patch, axis_name=dev_axis), axis_name=ax_name)]
  transfers between devices with their start and end apart: 5 -> 6, of which waited for: 4 -> 5; matrix products, arithmetic and copies ran while one was open for 14% -> 13% of each run, Pallas kernels for 0% -> 0%
where the time goes in v1:
time: 847 us; the launch traced here: 843 us
  waiting for transfers between devices  614 us (72%)
  other arithmetic  98.5 us (12%)
  local copies, waits for them, and re-layouts  75.1 us (9%)
  matrix products  40 us (5%)
  between operations  14.8 us (2%)
    psum x2, waiting for transfers between devices, stacks_all_resolve(): return lax.psum(lax.psum(patch, axis_name=dev_axis), axis_name=ax_name)  308 us
    psum x1, waiting for transfers between devices, body(): summed = lax.psum(partial_value, 'col')  153 us
    reduce_scatter x1, waiting for transfers between devices, body(): lax.psum_scatter(back_partial, 'row', scatter_dimension=0, tiled=True)  94.2 us
    all_gather x1, waiting for transfers between devices, body(): proj_block = lax.all_gather(projected, 'row', axis=0, tiled=True)  58.8 us
    scatter-add x1, other arithmetic, body(): jax.ops.segment_sum(products, fwd_targets, tile_rows + 1)[:tile_rows]  46 us
    scatter-add x1, other arithmetic, body(): jax.ops.segment_sum(back_products, back_targets, tile_cols + 1)[:tile_cols]  46 us
    dot_general x1, local copies, waits for them, and re-layouts, body(): jnp.einsum('tij,tjf->tif', tile_vals, gathered, preferred_element_type=jn...  23.5 us
    dot_general x1, local copies, waits for them, and re-layouts, body(): jnp.einsum('tji,tjf->tif', tile_vals, grad_tiles, preferred_element_type=...  23.5 us
  transfers between devices with their start and end apart: 6, of which 5 were waited for; matrix products, arithmetic and copies ran while one was open for 13% of the time, Pallas kernels for 0%

profile of v1, /device:TPU:1, one launch (start us, length us, event | category | flops | bytes accessed | tf_op | source)
XLA Modules:
  0.0 843.4 jit_solution(18120193965231730082)
XLA Ops:
  7.2 0.8 copy-done
  8.0 1.5 convolution_convert_fusion.1
  11.7 0.7 fusion.13
  12.4 58.8 %all-gather.3.cloned.1.call-done = bf16[4096,128]{1,0:T(8,128)(2,1)} async-done(((bf16[256,128]{1,0:T(8,128)(2,1)}), bf16[4096,128]{1,0:T(8,128)(2,1)}) %all-gather.3.cloned.1.call-update) | async-done | bytes 1048592 | tf_op jit(solution)/shard_map/all_gather | solution.py:31
  71.3 12.2 %gather_fusion = bf16[352,128,128]{2,1,0:T(8,128)(2,1)} fusion(bf16[32,128,128]{2,1,0:T(8,128)(2,1)} %bitcast.41, s32[1024]{0:T(1024)S(1)} %pad_clamp_fusion.1), kind=kCustom, calls=%fused_computation | custom fusion | bytes 23070080 | tf_op jit(solution)/shard_map/gather | solution.py:33
  83.5 20.6 %fusion.4 = f32[352,128,128]{1,2,0:T(8,128)} fusion(bf16[352,128,128]{2,1,0:T(8,128)(2,1)} %gather_fusion, bf16[1,1,352,128,128]{4,3,2,1,0:T(8,128)(2,1)} %param.8), kind=kOutput, calls=%fused_computation.8 | convolution fusion | flops 1476395008 | bytes 46137344 | tf_op jit(solution)/shard_map/tij,tjf->tif/dot_general | solution.py:34
  104.1 23.5 %copy.13 = f32[352,128,128]{2,1,0:T(8,128)} copy(f32[352,128,128]{1,2,0:T(8,128)} %fusion.4) | data formatting | bytes 46137344 | tf_op jit(solution)/shard_map/tij,tjf->tif/dot_general | solution.py:34
  127.8 46.0 %scatter_fusion = f32[33,128,128]{2,1,0:T(8,128)S(1)} fusion(f32[33,128,128]{2,1,0:T(8,128)S(1)} %broadcast.191.clone, s32[352]{0:T(512)S(1)} %get-tuple-element.10, f32[352,128,128]{2,1,0:T(8,128)} %copy.13), kind=kCustom, calls=%fused_computation.2 | custom fusion | flops 5767168 | bytes 69207424 | tf_op jit(solution)/shard_map/scatter-add | solution.py:36
  173.9 1.5 slice.12
  175.7 153.0 %all-reduce.4.cloned.1.call-done = f32[4096,128]{1,0:T(8,128)} async-done(((f32[4096,128]{1,0:T(8,128)}), f32[4096,128]{1,0:T(8,128)}) %all-reduce.4.cloned.1.call-update) | async-done | bytes 2097168 | tf_op jit(solution)/shard_map/psum | solution.py:39
  328.6 2.6 multiply_convert_fusion
  331.3 11.0 %gather_fusion.1 = bf16[352,128,128]{2,1,0:T(8,128)(2,1)} fusion(bf16[32,128,128]{2,1,0:T(8,128)(2,1)S(1)} %bitcast.40, s32[1024]{0:T(1024)S(1)} %pad_clamp_fusion), kind=kCustom, calls=%fused_computation.1 | custom fusion | bytes 23070080 | tf_op jit(solution)/shard_map/gather | solution.py:44
  342.3 14.4 %fusion.7 = f32[352,128,128]{1,2,0:T(8,128)} fusion(bf16[352,128,128]{2,1,0:T(8,128)(2,1)} %gather_fusion.1, bf16[1,1,352,128,128]{4,3,2,1,0:T(8,128)(2,1)} %param.8), kind=kOutput, calls=%fused_computation.9 | convolution fusion | flops 1476395008 | bytes 46137344 | tf_op jit(solution)/shard_map/tji,tjf->tif/dot_general | solution.py:45
  356.7 23.5 %copy.15 = f32[352,128,128]{2,1,0:T(8,128)} copy(f32[352,128,128]{1,2,0:T(8,128)} %fusion.7) | data formatting | bytes 46137344 | tf_op jit(solution)/shard_map/tji,tjf->tif/dot_general | solution.py:45
  380.4 46.0 %scatter_fusion.1 = f32[33,128,128]{2,1,0:T(8,128)S(1)} fusion(f32[33,128,128]{2,1,0:T(8,128)S(1)} %broadcast.191, s32[352]{0:T(512)S(1)} %get-tuple-element.11, f32[352,128,128]{2,1,0:T(8,128)} %copy.15), kind=kCustom, calls=%fused_computation.3 | custom fusion | flops 5767168 | bytes 69207424 | tf_op jit(solution)/shard_map/scatter-add | solution.py:49
  426.4 1.5 slice.13
  428.0 94.2 %reduce-scatter.2.cloned.1.call-done = f32[256,128]{1,0:T(8,128)} async-done(((f32[4096,128]{1,0:T(8,128)}), f32[256,128]{1,0:T(8,128)}) %reduce-scatter.2.cloned.1.call-update) | async-done | bytes 131088 | tf_op jit(solution)/shard_map/reduce_scatter | solution.py:52
  522.2 1.7 convolution_bitcast_fusion
  524.0 1.6 multiply_convert_fusion.1
  525.6 136.4 %all-reduce.6.cloned.1.call-done = f32[128,128]{0,1:T(8,128)} async-done(((f32[128,128]{0,1:T(8,128)}), f32[128,128]{0,1:T(8,128)}) %all-reduce.6.cloned.1.call-update) | async-done | bytes 65552 | tf_op jit(solution)/shard_map/psum | solution.py:16
  662.0 1.7 convolution_convert_fusion
  663.7 171.3 %all-reduce.8.cloned.1.call-done = f32[128,128]{0,1:T(8,128)} async-done(((f32[128,128]{0,1:T(8,128)}), f32[128,128]{0,1:T(8,128)}) %all-reduce.8.cloned.1.call-update) | async-done | bytes 65552 | tf_op jit(solution)/shard_map/psum | solution.py:16
  835.0 0.8 broadcast_multiply_fusion
  835.8 0.7 copy.16
  (21 shorter events, 2.4 us)
Async XLA Ops:
  7.2 0.8 copy-start
  7.2 64.1 %all-gather.3.cloned.1.call-start = ((), (), s32[]{:S(2)}) async-start(), calls=%async_computation.1 | async-start | bytes 1114112 | tf_op jit(solution)/shard_map/all_gather | solution.py:31
  9.6 166.1 %all-gather.5.cloned.1.call-start = ((), (), s32[]{:S(2)}) async-start(), calls=%async_computation.3 | async-start | bytes 1114112 | tf_op jit(solution)/shard_map/all_gather | solution.py:42
  10.3 318.3 %all-reduce.4.cloned.1.call-start = ((), (), s32[]{:S(2)}) async-start(), calls=%async_computation.2 | async-start | bytes 4194304 | tf_op jit(solution)/shard_map/psum | solution.py:39
  175.4 346.8 %reduce-scatter.2.cloned.1.call-start = ((), (), s32[]{:S(2)}) async-start(), calls=%async_computation.4 | async-start | bytes 2228224 | tf_op jit(solution)/shard_map/reduce_scatter | solution.py:52
  380.4 281.6 %copy-start.1 = (bf16[128,128]{1,0:T(8,128)(2,1)S(1)}, bf16[128,128]{1,0:T(8,128)(2,1)}, u32[]{:S(2)}) copy-start(bf16[128,128]{1,0:T(8,128)(2,1)} %param.7) | copy-start | bytes 98308
  428.0 234.0 %all-reduce.6.cloned.1.call-start = ((), (), s32[]{:S(2)}) async-start(), calls=%async_computation.5 | async-start | bytes 131072 | tf_op jit(solution)/shard_map/psum | solution.py:16
  523.9 311.0 %all-reduce.8.cloned.1.call-start = ((), (), s32[]{:S(2)}) async-start(), calls=%async_computation.6 | async-start | bytes 131072 | tf_op jit(solution)/shard_map/psum | solution.py:16
Sparse Core Ops, SparseCore 0:
  11.3 59.9 all-gather.2
  73.1 65.9 all-gather.4
  175.5 153.0 all-reduce.3
  428.1 94.0 reduce-scatter.1
  525.2 136.6 all-reduce.5
  664.6 170.3 all-reduce.7
